TPU v7x, 32 devices: a whole 2x2x4 slice. The times are simulated.
32 devices in a mesh: expert: 4 (over x, core), group: 8 (over z, y).
Axes of the slice: x: 2, y: 2, z: 4, core: 2. Of those that a mesh axis runs over, the one named last changes fastest.
Arguments:
- tokens: bfloat16 [16384, 2048], P(('expert', 'group')), may hold values from -6 to 6
- routing: int32 [16384, 8], P(('expert', 'group')), may hold values from 0 to 31, as said below
- mixing: float32 [16384, 8], P(('expert', 'group')), may hold values from 0.1 to 1
- visited: int32 [4], replicated, may hold values from 0 to 31, as said below
- gate_matrix: bfloat16 [32, 2048, 768], P('expert', 'group'), may hold values from -0.125 to 0.125
- up_matrix: bfloat16 [32, 2048, 768], P('expert', 'group'), may hold values from -0.125 to 0.125
- down_matrix: bfloat16 [32, 768, 2048], P('expert', None, 'group'), may hold values from -0.21875 to 0.21875
Outputs:
- combined: bfloat16 [16384, 2048], P(('expert', 'group'))
Inputs may be any that keep to these rules, and one draw needn't show every extreme that they name: `routing`: each row names 8 different experts. In the rows of one device, each expert of visited is named by at least half of 80 (rounded up) and at most 80 rows, and for each visited expert some device has exactly 80 such rows. `visited`: 4 different experts.
All inputs are finite; a program needn't handle non-finite values.
Results may differ from a plain program's by a relative error of at most 0.0049.
Values may be sent and summed in bfloat16 or wider, within the bound.
No kernel may reach another device: no remote copies, remote signals or barrier semaphores. Data moves between devices by JAX's collectives and lax.ppermute only.
A program may use at most 128 MiB of HBM per device.

v0:
```python
import jax
import jax.numpy as jnp
from jax import lax
from jax.sharding import PartitionSpec as P

VISITS = 4
CAP = 80


def from_root(value, axis, source):
    kept = jnp.where(lax.axis_index(axis) == source, value, 0).astype(value.dtype)
    return lax.psum(kept, axis)


def select_rows(routing, mixing, target, capacity):
    hit = routing == target
    member = jnp.any(hit, axis=1)
    share = jnp.sum(jnp.where(hit, mixing, jnp.zeros_like(mixing)), axis=1)
    place = jnp.cumsum(member.astype(jnp.int32)) - 1
    slots = jnp.arange(capacity, dtype=jnp.int32)
    table = member[:, None] & (place[:, None] == slots[None, :])
    indices = jnp.arange(routing.shape[0], dtype=jnp.int32)
    rows = jnp.sum(jnp.where(table, indices[:, None], 0), axis=0)
    filled = jnp.any(table, axis=0)
    scales = jnp.where(filled, share[rows], jnp.zeros_like(share[rows]))
    return (rows, scales)


def body(tokens, routing, mixing, visited, gate_matrix, up_matrix, down_matrix):
    held = gate_matrix.shape[0]
    combined = jnp.zeros(tokens.shape, jnp.float32)
    for number in range(VISITS):
        target = visited[number]
        rows, scales = select_rows(routing, mixing, target, CAP)
        picked = tokens[rows]
        owner = target // held
        local = target % held
        slices = (
            lax.dynamic_index_in_dim(gate_matrix, local, 0, keepdims=False),
            lax.dynamic_index_in_dim(up_matrix, local, 0, keepdims=False),
            lax.dynamic_index_in_dim(down_matrix, local, 0, keepdims=False),
        )
        gate_slice, up_slice, down_slice = (
            from_root(slices[0], "expert", owner),
            from_root(slices[1], "expert", owner),
            from_root(slices[2], "expert", owner),
        )
        empty = jnp.zeros((CAP, gate_slice.shape[1]), jnp.float32)

        def add_both(totals, pieces, start, picked=picked):
            return (
                jnp.dot(picked, pieces[0], preferred_element_type=jnp.float32),
                jnp.dot(picked, pieces[1], preferred_element_type=jnp.float32),
            )

        gate, up = add_both(
            (empty, empty),
            (
                lax.all_gather(gate_slice, "group", axis=0, tiled=True),
                lax.all_gather(up_slice, "group", axis=0, tiled=True),
            ),
            jnp.int32(0),
        )
        hidden = (jax.nn.silu(gate) * up).astype(jnp.bfloat16)

        def partial_columns(piece, start, down_slice=down_slice):
            return jnp.dot(piece, down_slice, preferred_element_type=jnp.float32)

        column_parts = partial_columns(
            lax.all_gather(hidden, "group", axis=0, tiled=True), jnp.int32(0)
        )
        expert_output = lax.all_to_all(
            column_parts, "group", split_axis=0, concat_axis=1, tiled=True
        )
        combined = combined.at[rows].add(scales[:, None] * expert_output)
    return combined.astype(jnp.bfloat16)


def solution(mesh):
    placed = (
        P(("expert", "group"), None),
        P(("expert", "group"), None),
        P(("expert", "group"), None),
        P(),
        P("expert", "group", None),
        P("expert", "group", None),
        P("expert", None, "group"),
    )
    return jax.shard_map(
        body, mesh=mesh, in_specs=placed, out_specs=P(("expert", "group"), None), check_vma=False
    )
```

profile of v0, /device:TPU:0, one launch (start us, length us, event | category | flops | bytes accessed | tf_op | source)
XLA Modules:
  0.0 753.0 jit_solution(4360539912461578354)
XLA Ops:
  6.5 1.5 fusion.32
  18.0 2.7 select_bitcast_fusion
  20.7 3.0 select_bitcast_fusion.1
  23.8 97.0 %all-reduce.3.cloned.1.call-done = (bf16[256,768]{1,0:T(8,128)(2,1)}, bf16[256,768]{1,0:T(8,128)(2,1)}, bf16[768,256]{1,0:T(8,128)(2,1)}, bf16[256,768]{1,0:T(8,...) async-done(((bf16[256,768]{1,0:T(8,128)(2,1)}, ...) | async-done | bytes 4718608 | tf_op jit(solution)/shard_map/psum | solution.py:12
  120.9 0.7 all-gather.15.cloned.1.call-update
  121.7 0.5 all-gather.9.cloned.1.call-update
  122.2 0.5 all-gather.11.cloned.1.call-update
  122.8 0.5 all-gather.17.cloned.1.call-update
  123.4 0.7 all-gather.19.cloned.1.call-update
  124.1 0.7 all-gather.21.cloned.1.call-update
  124.9 1.9 fusion.30
  126.8 0.6 select_reduce_fusion.4
  127.5 0.3 reduce-window.34
  127.9 0.3 reduce-window.36
  128.3 0.3 reduce-window.50
  128.7 0.3 reduce-window.48
  129.2 0.2 slice_reduce_fusion.2
  129.8 0.1 select_reduce_fusion.3
  130.1 0.8 gather_fusion.3
  130.9 0.8 gather_fusion.1
  131.8 0.2 select_reduce_fusion
  131.9 0.8 gather_fusion.5
  132.8 0.8 gather_fusion.7
  133.7 49.8 %all-gather.13.cloned.1.call-done = bf16[2048,768]{1,0:T(8,128)(2,1)} async-done(((bf16[256,768]{1,0:T(8,128)(2,1)}), bf16[2048,768]{1,0:T(8,128)(2,1)}) %all-gather.13.cloned.1.call-update) | async-done | bytes 3145744 | tf_op jit(solution)/shard_map/all_gather | solution.py:59
  183.5 2.5 fusion.35
  186.0 58.4 %all-gather.15.cloned.1.call-done = bf16[2048,768]{1,0:T(8,128)(2,1)} async-done(((bf16[256,768]{1,0:T(8,128)(2,1)}), bf16[2048,768]{1,0:T(8,128)(2,1)}) %all-gather.15.cloned.1.call-update) | async-done | bytes 3145744 | tf_op jit(solution)/shard_map/all_gather | solution.py:60
  244.4 2.5 fusion.3
  246.9 34.9 %all_gather.41 = bf16[640,768]{1,0:T(8,128)(2,1)S(1)} all-gather(bf16[80,768]{1,0:T(8,128)(2,1)S(1)} %fusion.3), channel_id=1, replica_groups=mesh['expert'=4,'group'=8] {'group'}, dimensions={0}, use_global_device_ids=true | all-gather | bytes 1105920 | tf_op jit(solution)/shard_map/all_gather | solution.py:70
  281.8 1.3 fusion.36
  283.1 3.5 all-to-all-start.1
  286.6 37.5 %all-gather.9.cloned.1.call-done = bf16[2048,768]{1,0:T(8,128)(2,1)} async-done(((bf16[256,768]{1,0:T(8,128)(2,1)}), bf16[2048,768]{1,0:T(8,128)(2,1)}) %all-gather.9.cloned.1.call-update) | async-done | bytes 3145744 | tf_op jit(solution)/shard_map/all_gather | solution.py:59
  324.2 2.5 fusion.33
  326.7 58.5 %all-gather.11.cloned.1.call-done = bf16[2048,768]{1,0:T(8,128)(2,1)} async-done(((bf16[256,768]{1,0:T(8,128)(2,1)}), bf16[2048,768]{1,0:T(8,128)(2,1)}) %all-gather.11.cloned.1.call-update) | async-done | bytes 3145744 | tf_op jit(solution)/shard_map/all_gather | solution.py:60
  385.2 2.5 fusion.2
  387.8 34.9 %all_gather.38 = bf16[640,768]{1,0:T(8,128)(2,1)S(1)} all-gather(bf16[80,768]{1,0:T(8,128)(2,1)S(1)} %fusion.2), channel_id=1, replica_groups=mesh['expert'=4,'group'=8] {'group'}, dimensions={0}, use_global_device_ids=true | all-gather | bytes 1105920 | tf_op jit(solution)/shard_map/all_gather | solution.py:70
  422.7 1.3 fusion.34
  423.9 3.5 all-to-all-start
  427.5 37.6 %all-gather.17.cloned.1.call-done = bf16[2048,768]{1,0:T(8,128)(2,1)} async-done(((bf16[256,768]{1,0:T(8,128)(2,1)}), bf16[2048,768]{1,0:T(8,128)(2,1)}) %all-gather.17.cloned.1.call-update) | async-done | bytes 3145744 | tf_op jit(solution)/shard_map/all_gather | solution.py:59
  465.1 2.5 fusion.37
  467.6 58.7 %all-gather.19.cloned.1.call-done = bf16[2048,768]{1,0:T(8,128)(2,1)} async-done(((bf16[256,768]{1,0:T(8,128)(2,1)}), bf16[2048,768]{1,0:T(8,128)(2,1)}) %all-gather.19.cloned.1.call-update) | async-done | bytes 3145744 | tf_op jit(solution)/shard_map/all_gather | solution.py:60
  526.3 2.6 fusion.4
  528.9 34.9 %all_gather.44 = bf16[640,768]{1,0:T(8,128)(2,1)S(1)} all-gather(bf16[80,768]{1,0:T(8,128)(2,1)S(1)} %fusion.4), channel_id=1, replica_groups=mesh['expert'=4,'group'=8] {'group'}, dimensions={0}, use_global_device_ids=true | all-gather | bytes 1105920 | tf_op jit(solution)/shard_map/all_gather | solution.py:70
  563.8 1.3 fusion.38
  565.0 4.2 all-to-all-start.2
  569.2 37.3 %all-gather.21.cloned.1.call-done = bf16[2048,768]{1,0:T(8,128)(2,1)} async-done(((bf16[256,768]{1,0:T(8,128)(2,1)}), bf16[2048,768]{1,0:T(8,128)(2,1)}) %all-gather.21.cloned.1.call-update) | async-done | bytes 3145744 | tf_op jit(solution)/shard_map/all_gather | solution.py:59
  606.6 2.5 fusion.39
  609.1 58.7 %all-gather.23.cloned.1.call-done = bf16[2048,768]{1,0:T(8,128)(2,1)} async-done(((bf16[256,768]{1,0:T(8,128)(2,1)}), bf16[2048,768]{1,0:T(8,128)(2,1)}) %all-gather.23.cloned.1.call-update) | async-done | bytes 3145744 | tf_op jit(solution)/shard_map/all_gather | solution.py:60
  667.8 2.6 fusion.5
  670.4 32.8 %all_gather.47 = bf16[640,768]{1,0:T(8,128)(2,1)S(1)} all-gather(bf16[80,768]{1,0:T(8,128)(2,1)S(1)} %fusion.5), channel_id=1, replica_groups=mesh['expert'=4,'group'=8] {'group'}, dimensions={0}, use_global_device_ids=true | all-gather | bytes 1105920 | tf_op jit(solution)/shard_map/all_gather | solution.py:70
  703.1 1.3 fusion.40
  704.4 3.7 all-to-all-start.3
  708.3 1.3 gather_fusion
  709.5 1.3 gather_fusion.2
  710.8 1.3 gather_fusion.4
  712.1 1.3 gather_fusion.6
  713.8 1.1 copy.22
  714.9 4.6 all-to-all-done.3
  719.6 0.8 copy-done.2
  720.4 1.1 copy.23
  721.5 3.8 scatter_custom_fusion
  725.4 5.7 scatter_custom_fusion.1
  731.1 5.7 scatter_custom_fusion.2
  736.8 5.9 scatter_custom_fusion.3
  742.7 3.8 convert_element_type.69
  (72 shorter events, 2.2 us)
Async XLA Ops:
  6.5 123.6 %copy-start = (bf16[512,2048]{1,0:T(8,128)(2,1)S(1)}, bf16[512,2048]{1,0:T(8,128)(2,1)}, u32[]{:S(2)}) copy-start(bf16[512,2048]{1,0:T(8,128)(2,1)} %param.7) | copy-start | bytes 6291460
  6.5 114.3 %all-reduce.3.cloned.1.call-start = ((), (), s32[]{:S(2)}) async-start(), calls=%async_computation.12 | async-start | bytes 9437184 | tf_op jit(solution)/shard_map/psum | solution.py:12
  18.0 2.7 copy-start.3
  23.7 101.2 %copy-start.8 = (s32[512,8]{0,1:T(8,128)S(1)}, s32[512,8]{0,1:T(8,128)}, u32[]{:S(2)}) copy-start(s32[512,8]{0,1:T(8,128)} %param.8) | copy-start | bytes 49156
  23.7 103.1 %copy-start.9 = (f32[512,8]{0,1:T(8,128)S(1)}, f32[512,8]{0,1:T(8,128)}, u32[]{:S(2)}) copy-start(f32[512,8]{0,1:T(8,128)} %param.9) | copy-start | bytes 49156
  23.8 159.7 %all-gather.13.cloned.1.call-start = ((), (), s32[]{:S(2)}) async-start(), calls=%async_computation.6 | async-start | bytes 3538944 | tf_op jit(solution)/shard_map/all_gather | solution.py:59
  120.9 123.5 %all-gather.15.cloned.1.call-start = ((), (), s32[]{:S(2)}) async-start(), calls=%async_computation.7 | async-start | bytes 3538944 | tf_op jit(solution)/shard_map/all_gather | solution.py:60
  121.6 202.6 %all-gather.9.cloned.1.call-start = ((), (), s32[]{:S(2)}) async-start(), calls=%async_computation.4 | async-start | bytes 3538944 | tf_op jit(solution)/shard_map/all_gather | solution.py:59
  122.2 263.1 %all-gather.11.cloned.1.call-start = ((), (), s32[]{:S(2)}) async-start(), calls=%async_computation.5 | async-start | bytes 3538944 | tf_op jit(solution)/shard_map/all_gather | solution.py:60
  122.8 342.3 %all-gather.17.cloned.1.call-start = ((), (), s32[]{:S(2)}) async-start(), calls=%async_computation.8 | async-start | bytes 3538944 | tf_op jit(solution)/shard_map/all_gather | solution.py:59
  123.3 402.9 %all-gather.19.cloned.1.call-start = ((), (), s32[]{:S(2)}) async-start(), calls=%async_computation.9 | async-start | bytes 3538944 | tf_op jit(solution)/shard_map/all_gather | solution.py:60
  124.1 482.5 %all-gather.21.cloned.1.call-start = ((), (), s32[]{:S(2)}) async-start(), calls=%async_computation.10 | async-start | bytes 3538944 | tf_op jit(solution)/shard_map/all_gather | solution.py:59
  124.8 542.9 %all-gather.23.cloned.1.call-start = ((), (), s32[]{:S(2)}) async-start(), calls=%async_computation.11 | async-start | bytes 3538944 | tf_op jit(solution)/shard_map/all_gather | solution.py:60
  186.0 95.8 %copy-start.7 = (bf16[768,256]{1,0:T(8,128)(2,1)S(1)}, bf16[768,256]{1,0:T(8,128)(2,1)}, u32[]{:S(2)}) copy-start(bf16[768,256]{1,0:T(8,128)(2,1)} %get-tuple-element.14) | copy-start | bytes 1179652
  283.1 140.9 %all-to-all-start.1 = ((f32[8,80,256]{2,1,0:T(8,128)}), f32[8,80,256]{2,1,0:T(8,128)S(1)}, u32[]{:S(2)}, u32[]{:S(2)}) async-start(f32[8,80,256]{2,1,0:T(8,128)} %bitcast.108), calls=%async_computation.1 | async-start | bytes 1310720 | tf_op jit(solution)/shard_map/all_to_all | solution.py:72
  326.7 96.0 %copy-start.6 = (bf16[768,256]{1,0:T(8,128)(2,1)S(1)}, bf16[768,256]{1,0:T(8,128)(2,1)}, u32[]{:S(2)}) copy-start(bf16[768,256]{1,0:T(8,128)(2,1)} %get-tuple-element.11) | copy-start | bytes 1179652
  423.9 141.1 %all-to-all-start = ((f32[8,80,256]{2,1,0:T(8,128)}), f32[8,80,256]{2,1,0:T(8,128)S(1)}, u32[]{:S(2)}, u32[]{:S(2)}) async-start(f32[8,80,256]{2,1,0:T(8,128)} %bitcast.107), calls=%async_computation | async-start | bytes 1310720 | tf_op jit(solution)/shard_map/all_to_all | solution.py:72
  526.3 37.5 %copy-start.5 = (bf16[768,256]{1,0:T(8,128)(2,1)S(1)}, bf16[768,256]{1,0:T(8,128)(2,1)}, u32[]{:S(2)}) copy-start(bf16[768,256]{1,0:T(8,128)(2,1)} %get-tuple-element.17) | copy-start | bytes 1179652
  565.0 139.4 %all-to-all-start.2 = ((f32[8,80,256]{2,1,0:T(8,128)}), f32[8,80,256]{2,1,0:T(8,128)}, u32[]{:S(2)}, u32[]{:S(2)}) async-start(f32[8,80,256]{2,1,0:T(8,128)} %bitcast.106), calls=%async_computation.2 | async-start | bytes 1310720 | tf_op jit(solution)/shard_map/all_to_all | solution.py:72
  667.8 35.3 %copy-start.4 = (bf16[768,256]{1,0:T(8,128)(2,1)S(1)}, bf16[768,256]{1,0:T(8,128)(2,1)}, u32[]{:S(2)}) copy-start(bf16[768,256]{1,0:T(8,128)(2,1)} %get-tuple-element.20) | copy-start | bytes 1179652
  704.4 15.2 %all-to-all-start.3 = ((f32[8,80,256]{2,1,0:T(8,128)}), f32[8,80,256]{2,1,0:T(8,128)S(1)}, u32[]{:S(2)}, u32[]{:S(2)}) async-start(f32[8,80,256]{2,1,0:T(8,128)} %bitcast.38), calls=%async_computation.3 | async-start | bytes 1310720 | tf_op jit(solution)/shard_map/all_to_all | solution.py:72
  719.6 0.8 copy-start.2
  736.8 9.7 %copy-start.1 = (bf16[512,2048]{1,0:T(8,128)(2,1)S(1)}, bf16[512,2048]{1,0:T(8,128)(2,1)}, u32[]{:S(2)}) copy-start(bf16[512,2048]{1,0:T(8,128)(2,1)} %param.7) | copy-start | bytes 6291460
Sparse Core Ops, SparseCore 0:
  23.9 96.9 all-reduce.2
  123.0 60.3 all-gather.12
  185.7 58.6 all-gather.14
  246.4 77.7 all-gather.8
  326.2 58.9 all-gather.10
  387.3 77.7 all-gather.16
  467.2 58.9 all-gather.18
  528.5 78.0 all-gather.20
  608.8 58.9 all-gather.22
where the time goes:
time: 754 us; the launch traced here: 753 us
  waiting for transfers between devices  502 us (67%)
  blocking collectives  137 us (18%)
  other arithmetic  35.9 us (5%)
  matrix products  25.4 us (3%)
  between operations  23.4 us (3%)
  starting transfers between devices  15.3 us (2%)
  local copies, waits for them, and re-layouts  13.7 us (2%)
    all_gather x4, waiting for transfers between devices, body(): lax.all_gather(up_slice, 'group', axis=0, tiled=True)  234 us
    all_gather x4, waiting for transfers between devices, body(): lax.all_gather(gate_slice, 'group', axis=0, tiled=True)  162 us
    all_gather x4, blocking collectives, body(): lax.all_gather(hidden, 'group', axis=0, tiled=True)  137 us
    psum x1, waiting for transfers between devices, from_root(): return lax.psum(kept, axis)  97 us
    scatter-add x4, other arithmetic, body(): combined = combined.at[rows].add(scales[:, None] * expert_output)  21.1 us
  transfers between devices with their start and end apart: 13, of which 10 were waited for; matrix products, arithmetic and copies ran while one was open for 5% of the time, Pallas kernels for 0%

commit v1 on v0

--- a/solution.py
+++ b/solution.py
@@ -9,7 +9,7 @@
 
 def from_root(value, axis, source):
     kept = jnp.where(lax.axis_index(axis) == source, value, 0).astype(value.dtype)
-    return lax.psum(kept, axis)
+    return jnp.sum(lax.all_gather(kept, axis), axis=0)
 
 
 def select_rows(routing, mixing, target, capacity):

time: 754 us -> 909 us (1.21)
  waiting for transfers between devices: 502 us -> 624 us
  other arithmetic: 35.9 us -> 66.4 us
    all_gather x0 -> x12, waiting for transfers between devices: none -> 208 us  [from_root(): return jnp.sum(lax.all_gather(kept, axis), axis=0)]
    psum x1 -> x0, waiting for transfers between devices: 97 us -> none  [from_root(): return lax.psum(kept, axis)]
    reduce_sum x0 -> x12, other arithmetic: none -> 28.6 us  [from_root(): return jnp.sum(lax.all_gather(kept, axis), axis=0)]
    all_gather x4, waiting for transfers between devices: 162 us -> 173 us  [body(): lax.all_gather(gate_slice, 'group', axis=0, tiled=True)]
  transfers between devices with their start and end apart: 13 -> 24, of which waited for: 10 -> 21; matrix products, arithmetic and copies ran while one was open for 5% -> 8% of each run, Pallas kernels for 0% -> 0%
where the time goes in v1:
time: 909 us; the launch traced here: 908 us
  waiting for transfers between devices  624 us (69%)
  blocking collectives  137 us (15%)
  other arithmetic  66.4 us (7%)
  matrix products  25.3 us (3%)
  between operations  24 us (3%)
  starting transfers between devices  15.8 us (2%)
  local copies, waits for them, and re-layouts  14.6 us (2%)
    all_gather x4, waiting for transfers between devices, body(): lax.all_gather(up_slice, 'group', axis=0, tiled=True)  234 us
    all_gather x12, waiting for transfers between devices, from_root(): return jnp.sum(lax.all_gather(kept, axis), axis=0)  208 us
    all_gather x4, waiting for transfers between devices, body(): lax.all_gather(gate_slice, 'group', axis=0, tiled=True)  173 us
    all_gather x4, blocking collectives, body(): lax.all_gather(hidden, 'group', axis=0, tiled=True)  137 us
    reduce_sum x12, other arithmetic, from_root(): return jnp.sum(lax.all_gather(kept, axis), axis=0)  28.6 us
    scatter-add x4, other arithmetic, body(): combined = combined.at[rows].add(scales[:, None] * expert_output)  21.1 us
  transfers between devices with their start and end apart: 24, of which 21 were waited for; matrix products, arithmetic and copies ran while one was open for 8% of the time, Pallas kernels for 0%

profile of v1, /device:TPU:0, one launch (start us, length us, event | category | flops | bytes accessed | tf_op | source)
XLA Modules:
  0.0 907.6 jit_solution(16596525335230926501)
XLA Ops:
  6.5 1.5 fusion.40
  18.0 2.5 dynamic-slice_select_fusion.2
  20.6 2.5 dynamic-slice_select_fusion.1
  27.2 2.6 dynamic-slice_select_fusion
  31.7 11.4 %all-gather.21.cloned.1.call-done = bf16[4,256,768]{2,1,0:T(8,128)(2,1)} async-done(((bf16[1,256,768]{2,1,0:T(8,128)(2,1)}), bf16[4,256,768]{2,1,0:T(8,128)(2,1)}) %all-gather.21.cloned.1.call-update) | async-done | bytes 1572880 | tf_op jit(solution)/shard_map/all_gather | solution.py:12
  43.1 2.5 reduce_sum.227
  45.7 18.7 %all-gather.25.cloned.1.call-done = bf16[4,256,768]{2,1,0:T(8,128)(2,1)} async-done(((bf16[1,256,768]{2,1,0:T(8,128)(2,1)}), bf16[4,256,768]{2,1,0:T(8,128)(2,1)}) %all-gather.25.cloned.1.call-update) | async-done | bytes 1572880 | tf_op jit(solution)/shard_map/all_gather | solution.py:12
  64.3 2.5 reduce_sum.228
  66.9 18.7 %all-gather.31.cloned.1.call-done = bf16[4,256,768]{2,1,0:T(8,128)(2,1)} async-done(((bf16[1,256,768]{2,1,0:T(8,128)(2,1)}), bf16[4,256,768]{2,1,0:T(8,128)(2,1)}) %all-gather.31.cloned.1.call-update) | async-done | bytes 1572880 | tf_op jit(solution)/shard_map/all_gather | solution.py:12
  85.6 2.5 reduce_sum.233
  88.1 18.5 %all-gather.35.cloned.1.call-done = bf16[4,256,768]{2,1,0:T(8,128)(2,1)} async-done(((bf16[1,256,768]{2,1,0:T(8,128)(2,1)}), bf16[4,256,768]{2,1,0:T(8,128)(2,1)}) %all-gather.35.cloned.1.call-update) | async-done | bytes 1572880 | tf_op jit(solution)/shard_map/all_gather | solution.py:12
  106.6 2.5 reduce_sum.234
  109.2 18.5 %all-gather.41.cloned.1.call-done = bf16[4,256,768]{2,1,0:T(8,128)(2,1)} async-done(((bf16[1,256,768]{2,1,0:T(8,128)(2,1)}), bf16[4,256,768]{2,1,0:T(8,128)(2,1)}) %all-gather.41.cloned.1.call-update) | async-done | bytes 1572880 | tf_op jit(solution)/shard_map/all_gather | solution.py:12
  127.7 2.5 reduce_sum.239
  130.3 18.5 %all-gather.45.cloned.1.call-done = bf16[4,256,768]{2,1,0:T(8,128)(2,1)} async-done(((bf16[1,256,768]{2,1,0:T(8,128)(2,1)}), bf16[4,256,768]{2,1,0:T(8,128)(2,1)}) %all-gather.45.cloned.1.call-update) | async-done | bytes 1572880 | tf_op jit(solution)/shard_map/all_gather | solution.py:12
  148.8 2.5 reduce_sum.240
  151.4 18.7 %all-gather.51.cloned.1.call-done = bf16[4,256,768]{2,1,0:T(8,128)(2,1)} async-done(((bf16[1,256,768]{2,1,0:T(8,128)(2,1)}), bf16[4,256,768]{2,1,0:T(8,128)(2,1)}) %all-gather.51.cloned.1.call-update) | async-done | bytes 1572880 | tf_op jit(solution)/shard_map/all_gather | solution.py:12
  170.0 2.5 reduce_sum.245
  172.6 1.9 fusion.38
  177.7 13.5 %all-gather.55.cloned.1.call-done = bf16[4,256,768]{2,1,0:T(8,128)(2,1)} async-done(((bf16[1,256,768]{2,1,0:T(8,128)(2,1)}), bf16[4,256,768]{2,1,0:T(8,128)(2,1)}) %all-gather.55.cloned.1.call-update) | async-done | bytes 1572880 | tf_op jit(solution)/shard_map/all_gather | solution.py:12
  191.2 2.5 reduce_sum.246
  197.4 15.1 %all-gather.29.cloned.1.call-done = bf16[4,768,256]{2,1,0:T(8,128)(2,1)} async-done(((bf16[1,768,256]{2,1,0:T(8,128)(2,1)}), bf16[4,768,256]{2,1,0:T(8,128)(2,1)}) %all-gather.29.cloned.1.call-update) | async-done | bytes 1572880 | tf_op jit(solution)/shard_map/all_gather | solution.py:12
  212.5 1.8 reduce_sum.229
  214.4 19.2 %all-gather.39.cloned.1.call-done = bf16[4,768,256]{2,1,0:T(8,128)(2,1)} async-done(((bf16[1,768,256]{2,1,0:T(8,128)(2,1)}), bf16[4,768,256]{2,1,0:T(8,128)(2,1)}) %all-gather.39.cloned.1.call-update) | async-done | bytes 1572880 | tf_op jit(solution)/shard_map/all_gather | solution.py:12
  233.6 2.5 reduce_sum.235
  236.1 18.7 %all-gather.49.cloned.1.call-done = bf16[4,768,256]{2,1,0:T(8,128)(2,1)} async-done(((bf16[1,768,256]{2,1,0:T(8,128)(2,1)}), bf16[4,768,256]{2,1,0:T(8,128)(2,1)}) %all-gather.49.cloned.1.call-update) | async-done | bytes 1572880 | tf_op jit(solution)/shard_map/all_gather | solution.py:12
  254.8 2.5 reduce_sum.241
  257.3 18.6 %all-gather.59.cloned.1.call-done = bf16[4,768,256]{2,1,0:T(8,128)(2,1)} async-done(((bf16[1,768,256]{2,1,0:T(8,128)(2,1)}), bf16[4,768,256]{2,1,0:T(8,128)(2,1)}) %all-gather.59.cloned.1.call-update) | async-done | bytes 1572880 | tf_op jit(solution)/shard_map/all_gather | solution.py:12
  275.9 1.8 reduce_sum.247
  277.7 60.4 %all-gather.23.cloned.1.call-done = bf16[2048,768]{1,0:T(8,128)(2,1)} async-done(((bf16[256,768]{1,0:T(8,128)(2,1)}), bf16[2048,768]{1,0:T(8,128)(2,1)}) %all-gather.23.cloned.1.call-update) | async-done | bytes 3145744 | tf_op jit(solution)/shard_map/all_gather | solution.py:59
  338.1 2.5 fusion.41
  340.7 58.2 %all-gather.27.cloned.1.call-done = bf16[2048,768]{1,0:T(8,128)(2,1)} async-done(((bf16[256,768]{1,0:T(8,128)(2,1)}), bf16[2048,768]{1,0:T(8,128)(2,1)}) %all-gather.27.cloned.1.call-update) | async-done | bytes 3145744 | tf_op jit(solution)/shard_map/all_gather | solution.py:60
  398.9 2.5 fusion.2
  401.4 34.9 %all_gather.88 = bf16[640,768]{1,0:T(8,128)(2,1)S(1)} all-gather(bf16[80,768]{1,0:T(8,128)(2,1)S(1)} %fusion.2), channel_id=1, replica_groups=mesh['expert'=4,'group'=8] {'group'}, dimensions={0}, use_global_device_ids=true | all-gather | bytes 1105920 | tf_op jit(solution)/shard_map/all_gather | solution.py:70
  437.6 3.5 all-to-all-start
  441.1 37.6 %all-gather.33.cloned.1.call-done = bf16[2048,768]{1,0:T(8,128)(2,1)} async-done(((bf16[256,768]{1,0:T(8,128)(2,1)}), bf16[2048,768]{1,0:T(8,128)(2,1)}) %all-gather.33.cloned.1.call-update) | async-done | bytes 3145744 | tf_op jit(solution)/shard_map/all_gather | solution.py:59
  478.7 2.5 fusion.42
  481.3 58.5 %all-gather.37.cloned.1.call-done = bf16[2048,768]{1,0:T(8,128)(2,1)} async-done(((bf16[256,768]{1,0:T(8,128)(2,1)}), bf16[2048,768]{1,0:T(8,128)(2,1)}) %all-gather.37.cloned.1.call-update) | async-done | bytes 3145744 | tf_op jit(solution)/shard_map/all_gather | solution.py:60
  539.8 2.5 fusion.3
  542.3 34.9 %all_gather.94 = bf16[640,768]{1,0:T(8,128)(2,1)S(1)} all-gather(bf16[80,768]{1,0:T(8,128)(2,1)S(1)} %fusion.3), channel_id=1, replica_groups=mesh['expert'=4,'group'=8] {'group'}, dimensions={0}, use_global_device_ids=true | all-gather | bytes 1105920 | tf_op jit(solution)/shard_map/all_gather | solution.py:70
  578.5 3.7 all-to-all-start.1
  582.2 37.4 %all-gather.43.cloned.1.call-done = bf16[2048,768]{1,0:T(8,128)(2,1)} async-done(((bf16[256,768]{1,0:T(8,128)(2,1)}), bf16[2048,768]{1,0:T(8,128)(2,1)}) %all-gather.43.cloned.1.call-update) | async-done | bytes 3145744 | tf_op jit(solution)/shard_map/all_gather | solution.py:59
  619.6 2.5 fusion.43
  622.1 58.5 %all-gather.47.cloned.1.call-done = bf16[2048,768]{1,0:T(8,128)(2,1)} async-done(((bf16[256,768]{1,0:T(8,128)(2,1)}), bf16[2048,768]{1,0:T(8,128)(2,1)}) %all-gather.47.cloned.1.call-update) | async-done | bytes 3145744 | tf_op jit(solution)/shard_map/all_gather | solution.py:60
  680.7 2.6 fusion.4
  683.3 34.9 %all_gather.100 = bf16[640,768]{1,0:T(8,128)(2,1)S(1)} all-gather(bf16[80,768]{1,0:T(8,128)(2,1)S(1)} %fusion.4), channel_id=1, replica_groups=mesh['expert'=4,'group'=8] {'group'}, dimensions={0}, use_global_device_ids=true | all-gather | bytes 1105920 | tf_op jit(solution)/shard_map/all_gather | solution.py:70
  718.2 1.3 fusion.15
  719.4 4.2 all-to-all-start.2
  723.6 37.4 %all-gather.53.cloned.1.call-done = bf16[2048,768]{1,0:T(8,128)(2,1)} async-done(((bf16[256,768]{1,0:T(8,128)(2,1)}), bf16[2048,768]{1,0:T(8,128)(2,1)}) %all-gather.53.cloned.1.call-update) | async-done | bytes 3145744 | tf_op jit(solution)/shard_map/all_gather | solution.py:59
  761.0 2.5 fusion.44
  763.5 58.5 %all-gather.57.cloned.1.call-done = bf16[2048,768]{1,0:T(8,128)(2,1)} async-done(((bf16[256,768]{1,0:T(8,128)(2,1)}), bf16[2048,768]{1,0:T(8,128)(2,1)}) %all-gather.57.cloned.1.call-update) | async-done | bytes 3145744 | tf_op jit(solution)/shard_map/all_gather | solution.py:60
  822.1 2.5 fusion.5
  824.6 32.8 %all_gather.106 = bf16[640,768]{1,0:T(8,128)(2,1)S(1)} all-gather(bf16[80,768]{1,0:T(8,128)(2,1)S(1)} %fusion.5), channel_id=1, replica_groups=mesh['expert'=4,'group'=8] {'group'}, dimensions={0}, use_global_device_ids=true | all-gather | bytes 1105920 | tf_op jit(solution)/shard_map/all_gather | solution.py:70
  858.6 3.5 all-to-all-start.3
  862.3 1.3 gather_fusion
  863.6 1.3 gather_fusion.2
  864.8 1.3 gather_fusion.4
  866.1 1.3 gather_fusion.6
  869.8 3.9 all-to-all-done.3
  875.8 3.8 scatter_custom_fusion
  879.6 5.7 scatter_custom_fusion.1
  885.3 5.7 scatter_custom_fusion.2
  891.0 5.9 scatter_custom_fusion.3
  896.9 3.8 convert_element_type.93
  (114 shorter events, 21.4 us)
Async XLA Ops:
  6.5 187.3 %copy-start = (bf16[512,2048]{1,0:T(8,128)(2,1)S(1)}, bf16[512,2048]{1,0:T(8,128)(2,1)}, u32[]{:S(2)}) copy-start(bf16[512,2048]{1,0:T(8,128)(2,1)} %param.7) | copy-start | bytes 6291460
  6.5 36.6 %all-gather.21.cloned.1.call-start = ((), (), s32[]{:S(2)}) async-start(), calls=%async_computation.4 | async-start | bytes 1966080 | tf_op jit(solution)/shard_map/all_gather | solution.py:12
  20.6 43.7 %all-gather.25.cloned.1.call-start = ((), (), s32[]{:S(2)}) async-start(), calls=%async_computation.6 | async-start | bytes 1966080 | tf_op jit(solution)/shard_map/all_gather | solution.py:12
  23.2 62.4 %all-gather.31.cloned.1.call-start = ((), (), s32[]{:S(2)}) async-start(), calls=%async_computation.9 | async-start | bytes 1966080 | tf_op jit(solution)/shard_map/all_gather | solution.py:12
  23.9 82.7 %all-gather.35.cloned.1.call-start = ((), (), s32[]{:S(2)}) async-start(), calls=%async_computation.11 | async-start | bytes 1966080 | tf_op jit(solution)/shard_map/all_gather | solution.py:12
  24.5 103.2 %all-gather.41.cloned.1.call-start = ((), (), s32[]{:S(2)}) async-start(), calls=%async_computation.14 | async-start | bytes 1966080 | tf_op jit(solution)/shard_map/all_gather | solution.py:12
  25.1 123.7 %all-gather.45.cloned.1.call-start = ((), (), s32[]{:S(2)}) async-start(), calls=%async_computation.16 | async-start | bytes 1966080 | tf_op jit(solution)/shard_map/all_gather | solution.py:12
  25.7 144.3 %all-gather.51.cloned.1.call-start = ((), (), s32[]{:S(2)}) async-start(), calls=%async_computation.19 | async-start | bytes 1966080 | tf_op jit(solution)/shard_map/all_gather | solution.py:12
  26.4 164.8 %all-gather.55.cloned.1.call-start = ((), (), s32[]{:S(2)}) async-start(), calls=%async_computation.21 | async-start | bytes 1966080 | tf_op jit(solution)/shard_map/all_gather | solution.py:12
  27.2 185.4 %all-gather.29.cloned.1.call-start = ((), (), s32[]{:S(2)}) async-start(), calls=%async_computation.8 | async-start | bytes 1966080 | tf_op jit(solution)/shard_map/all_gather | solution.py:12
  29.8 203.8 %all-gather.39.cloned.1.call-start = ((), (), s32[]{:S(2)}) async-start(), calls=%async_computation.13 | async-start | bytes 1966080 | tf_op jit(solution)/shard_map/all_gather | solution.py:12
  30.4 224.4 %all-gather.49.cloned.1.call-start = ((), (), s32[]{:S(2)}) async-start(), calls=%async_computation.18 | async-start | bytes 1966080 | tf_op jit(solution)/shard_map/all_gather | solution.py:12
  31.1 244.8 %all-gather.59.cloned.1.call-start = ((), (), s32[]{:S(2)}) async-start(), calls=%async_computation.23 | async-start | bytes 1966080 | tf_op jit(solution)/shard_map/all_gather | solution.py:12
  31.7 306.5 %all-gather.23.cloned.1.call-start = ((), (), s32[]{:S(2)}) async-start(), calls=%async_computation.5 | async-start | bytes 3538944 | tf_op jit(solution)/shard_map/all_gather | solution.py:59
  45.6 353.3 %all-gather.27.cloned.1.call-start = ((), (), s32[]{:S(2)}) async-start(), calls=%async_computation.7 | async-start | bytes 3538944 | tf_op jit(solution)/shard_map/all_gather | solution.py:60
  66.8 411.9 %all-gather.33.cloned.1.call-start = ((), (), s32[]{:S(2)}) async-start(), calls=%async_computation.10 | async-start | bytes 3538944 | tf_op jit(solution)/shard_map/all_gather | solution.py:59
  88.1 451.7 %all-gather.37.cloned.1.call-start = ((), (), s32[]{:S(2)}) async-start(), calls=%async_computation.12 | async-start | bytes 3538944 | tf_op jit(solution)/shard_map/all_gather | solution.py:60
  109.2 63.4 %copy-start.6 = (s32[512,8]{0,1:T(8,128)S(1)}, s32[512,8]{0,1:T(8,128)}, u32[]{:S(2)}) copy-start(s32[512,8]{0,1:T(8,128)} %param.8) | copy-start | bytes 49156
  109.2 65.4 %copy-start.7 = (f32[512,8]{0,1:T(8,128)S(1)}, f32[512,8]{0,1:T(8,128)}, u32[]{:S(2)}) copy-start(f32[512,8]{0,1:T(8,128)} %param.9) | copy-start | bytes 49156
  109.2 510.4 %all-gather.43.cloned.1.call-start = ((), (), s32[]{:S(2)}) async-start(), calls=%async_computation.15 | async-start | bytes 3538944 | tf_op jit(solution)/shard_map/all_gather | solution.py:59
  130.2 550.5 %all-gather.47.cloned.1.call-start = ((), (), s32[]{:S(2)}) async-start(), calls=%async_computation.17 | async-start | bytes 3538944 | tf_op jit(solution)/shard_map/all_gather | solution.py:60
  151.3 609.7 %all-gather.53.cloned.1.call-start = ((), (), s32[]{:S(2)}) async-start(), calls=%async_computation.20 | async-start | bytes 3538944 | tf_op jit(solution)/shard_map/all_gather | solution.py:59
  172.5 649.5 %all-gather.57.cloned.1.call-start = ((), (), s32[]{:S(2)}) async-start(), calls=%async_computation.22 | async-start | bytes 3538944 | tf_op jit(solution)/shard_map/all_gather | solution.py:60
  437.6 140.9 %all-to-all-start = ((f32[8,80,256]{2,1,0:T(8,128)}), f32[8,80,256]{2,1,0:T(8,128)S(1)}, u32[]{:S(2)}, u32[]{:S(2)}) async-start(f32[8,80,256]{2,1,0:T(8,128)} %fusion.19), calls=%async_computation | async-start | bytes 1310720 | tf_op jit(solution)/shard_map/all_to_all | solution.py:72
  481.3 96.0 %copy-start.5 = (bf16[768,256]{1,0:T(8,128)(2,1)S(1)}, bf16[768,256]{1,0:T(8,128)(2,1)}, u32[]{:S(2)}) copy-start(bf16[768,256]{1,0:T(8,128)(2,1)} %reduce_sum.235) | copy-start | bytes 1179652
  578.5 140.9 %all-to-all-start.1 = ((f32[8,80,256]{2,1,0:T(8,128)}), f32[8,80,256]{2,1,0:T(8,128)S(1)}, u32[]{:S(2)}, u32[]{:S(2)}) async-start(f32[8,80,256]{2,1,0:T(8,128)} %fusion.17), calls=%async_computation.1 | async-start | bytes 1310720 | tf_op jit(solution)/shard_map/all_to_all | solution.py:72
  680.7 37.5 %copy-start.4 = (bf16[768,256]{1,0:T(8,128)(2,1)S(1)}, bf16[768,256]{1,0:T(8,128)(2,1)}, u32[]{:S(2)}) copy-start(bf16[768,256]{1,0:T(8,128)(2,1)} %reduce_sum.241) | copy-start | bytes 1179652
  719.4 139.2 %all-to-all-start.2 = ((f32[8,80,256]{2,1,0:T(8,128)}), f32[8,80,256]{2,1,0:T(8,128)}, u32[]{:S(2)}, u32[]{:S(2)}) async-start(f32[8,80,256]{2,1,0:T(8,128)} %fusion.15), calls=%async_computation.2 | async-start | bytes 1310720 | tf_op jit(solution)/shard_map/all_to_all | solution.py:72
  858.6 15.2 %all-to-all-start.3 = ((f32[8,80,256]{2,1,0:T(8,128)}), f32[8,80,256]{2,1,0:T(8,128)S(1)}, u32[]{:S(2)}, u32[]{:S(2)}) async-start(f32[8,80,256]{2,1,0:T(8,128)} %fusion.13), calls=%async_computation.3 | async-start | bytes 1310720 | tf_op jit(solution)/shard_map/all_to_all | solution.py:72
  868.6 7.2 copy-start.3
  873.8 0.8 copy-start.2
  891.0 9.7 %copy-start.1 = (bf16[512,2048]{1,0:T(8,128)(2,1)S(1)}, bf16[512,2048]{1,0:T(8,128)(2,1)}, u32[]{:S(2)}) copy-start(bf16[512,2048]{1,0:T(8,128)(2,1)} %param.7) | copy-start | bytes 6291460
Sparse Core Ops, SparseCore 0:
  20.7 22.3 all-gather.20
  44.7 19.6 all-gather.24
  65.9 19.6 all-gather.30
  87.0 19.6 all-gather.34
  108.0 19.6 all-gather.40
  129.1 19.6 all-gather.44
  150.3 19.6 all-gather.50
  171.6 19.6 all-gather.54
  192.8 19.6 all-gather.28
  213.9 19.6 all-gather.38
  235.2 19.6 all-gather.48
  256.2 19.6 all-gather.58
  278.1 60.0 all-gather.22
  340.2 58.6 all-gather.26
  400.9 77.7 all-gather.32
  480.8 58.9 all-gather.36
  541.8 77.7 all-gather.42
  621.7 58.9 all-gather.46
  682.9 78.0 all-gather.52
  763.0 58.9 all-gather.56
